TPU v7x, 256 devices: a whole 4x4x8 slice. The times are simulated.
256 devices in a mesh: batch: 8 (over z), col: 32 (over y, x, core).
Axes of the slice: x: 4, y: 4, z: 8, core: 2. Of those that a mesh axis runs over, the one named last changes fastest.
Arguments:
- views: bfloat16 [2, 1024, 4096], P(None, 'batch', 'col'), may hold values from -132 to 132
- norm_scale_gain: float32 [4096], P('col'), may hold values from 0.5 to 1.5
- norm_shift_bias: float32 [4096], P('col'), may hold values from -3 to 3
- weight: bfloat16 [4096, 8192], P(None, 'col'), may hold values from -0.09375 to 0.09375
Outputs:
- loss: float32 [], replicated
- grad_weight: float32 [4096, 8192], P('batch', 'col')
- grad_gain: float32 [4096], P('col')
- grad_bias: float32 [4096], P('col')
- views_gradient: float32 [2, 1024, 4096], P(None, 'batch', 'col')
All inputs are finite; a program needn't handle non-finite values.
Results may differ from a plain program's by a relative error of at most 0.0027.
Values may be sent and summed in bfloat16 or wider, within the bound.
A program may use at most 64 MiB of HBM per device.

v0:
```python
import jax
import jax.numpy as jnp
from jax import lax
from jax.sharding import PartitionSpec as P

E = 8192
eps_norm = 1e-05
eps_std = 0.0001


def gelu_slope(preactivation):
    value, pullback = jax.vjp(lambda t: jax.nn.gelu(t, approximate=True), preactivation)
    return pullback(jnp.ones_like(value))[0]


def shards(views, norm_scale_gain, norm_shift_bias, weight):
    n_batch = lax.axis_size("batch")
    n_col = lax.axis_size("col")
    local_rows = views.shape[1]
    sample_count = local_rows * n_batch
    scale = sample_count * E / 128.0
    hidden_float = views.astype(jnp.float32)
    total = lax.psum(jnp.sum(hidden_float, axis=1), "batch")
    batch_average = total[:, None, :] / sample_count
    centred = hidden_float - batch_average
    spread = lax.psum(jnp.sum(centred * centred, axis=1), "batch")
    var = spread[:, None, :] / sample_count
    inverse_deviation = 1.0 / jnp.sqrt(var + eps_norm)
    normalised_input = (hidden_float - batch_average) * inverse_deviation
    preactivation = norm_scale_gain * normalised_input + norm_shift_bias
    act = jax.nn.gelu(preactivation, approximate=True).astype(jnp.bfloat16)
    act_full = lax.all_gather(act, "col", axis=2, tiled=True)
    z_local = jnp.einsum(
        "vrk,kj->vrj", act_full, weight, preferred_element_type=jnp.float32
    ).astype(jnp.bfloat16)
    z_all = lax.all_gather(z_local, "batch", axis=1, tiled=True)
    zf_all = z_all.astype(jnp.float32)
    zmean = jnp.mean(zf_all, axis=1, keepdims=True)
    zc_all = zf_all - zmean
    zvar = jnp.sum(zc_all * zc_all, axis=1, keepdims=True) / (sample_count - 1)
    std = jnp.sqrt(zvar + eps_std)
    zcb_all = zc_all.astype(jnp.bfloat16)
    offset = lax.axis_index("batch") * local_rows
    zc_loc = lax.dynamic_slice_in_dim(zc_all, offset, local_rows, 1)
    zcb_loc = zc_loc.astype(jnp.bfloat16)
    diag = jnp.sum(jnp.square(zcb_all.astype(jnp.float32)), axis=1, keepdims=True)
    kernel_part = jnp.einsum("vrj,vmj->vrm", zcb_loc, zcb_all, preferred_element_type=jnp.float32)
    kernel = lax.psum(kernel_part, "col")
    kernel_b = kernel.astype(jnp.bfloat16)
    denom = float((sample_count - 1) ** 2 * E)
    coef = 4.0 * scale / denom
    hinge_coef = 25.0 * scale / (2.0 * E * (sample_count - 1))
    mask = jnp.where(std < 1.0, 1.0, 0.0)
    moved = jnp.einsum("vrm,vmj->vrj", kernel_b, zcb_all, preferred_element_type=jnp.float32)
    g_cov = coef * (moved - zcb_loc.astype(jnp.float32) * diag)
    g_var = -hinge_coef * mask * zc_loc / std
    summed = g_cov + g_var
    col_total = lax.psum(jnp.sum(summed, axis=1), "batch")
    zf_loc = z_local.astype(jnp.float32)
    diff = zf_loc[0] - zf_loc[1]
    g_inv = 50.0 * scale / (sample_count * E) * diff
    dz = summed - col_total[:, None, :] / sample_count + jnp.stack([g_inv, -g_inv])
    dzb = dz.astype(jnp.bfloat16)
    inv_share = jnp.sum(diff * diff) / (sample_count * E)
    hinge_share = jnp.sum(jnp.maximum(1.0 - std, 0.0)) / (2 * E)
    block_share = jnp.sum(kernel * kernel) / denom
    diag_share = jnp.sum(diag * diag) / denom
    share = 25.0 * inv_share + (25.0 * hinge_share - diag_share) / n_batch + block_share / n_col
    loss = lax.psum(share, ("batch", "col"))
    d_act_t = lax.psum_scatter(
        jnp.einsum("kj,vrj->kvr", weight, dzb, preferred_element_type=jnp.float32),
        "col",
        scatter_dimension=0,
        tiled=True,
    )
    d_act = jnp.transpose(d_act_t, (1, 2, 0))
    grad_weight = lax.psum_scatter(
        jnp.einsum("vrk,vrj->kj", act_full, dzb, preferred_element_type=jnp.float32),
        "batch",
        scatter_dimension=0,
        tiled=True,
    )
    preactivation_gradient = d_act * gelu_slope(preactivation)
    bias_gradient_sum, gain_gradient_sum = lax.psum(
        (
            jnp.sum(preactivation_gradient, axis=1),
            jnp.sum(preactivation_gradient * normalised_input, axis=1),
        ),
        "batch",
    )
    grad_bias = jnp.sum(bias_gradient_sum, axis=0)
    grad_gain = jnp.sum(gain_gradient_sum, axis=0)
    views_gradient = (
        norm_scale_gain
        * (
            preactivation_gradient
            - bias_gradient_sum[:, None, :] / sample_count
            - normalised_input * gain_gradient_sum[:, None, :] / sample_count
        )
        * inverse_deviation
    )
    return (loss, grad_weight, grad_gain, grad_bias, views_gradient)


def solution(mesh):
    placed = (P(None, "batch", "col"), P("col"), P("col"), P(None, "col"))
    return jax.shard_map(
        shards,
        mesh=mesh,
        in_specs=placed,
        out_specs=(P(), P("batch", "col"), P("col"), P("col"), P(None, "batch", "col")),
        check_vma=False,
    )
```

profile of v0, /device:TPU:1, one launch (start us, length us, event | category | flops | bytes accessed | tf_op | source)
XLA Modules:
  0.0 430.3 jit_solution(8545685748164966906)
XLA Ops:
  7.2 0.0 copy-start
  7.2 0.0 all-gather.3.cloned.1.call-start
  7.2 1.0 convert_reduce_fusion.1
  8.2 17.3 %psum.49 = f32[2,128]{1,0:T(2,128)S(1)} all-reduce(f32[2,128]{1,0:T(2,128)S(1)} %convert_reduce_fusion.1), channel_id=1, replica_groups=mesh['batch'=8,'col'=32] {'batch'}, use_global_device_ids=true, to_apply=%region_1.0 | all-reduce | flops 256 | bytes 2048 | tf_op jit(solution)/shard_map/psum | solution.py:23
  25.5 0.9 fusion.32
  26.4 10.8 %psum.50 = f32[2,128]{1,0:T(2,128)S(1)} all-reduce(f32[2,128]{1,0:T(2,128)S(1)} %fusion.32), channel_id=1, replica_groups=mesh['batch'=8,'col'=32] {'batch'}, use_global_device_ids=true, to_apply=%region_3.0 | all-reduce | flops 256 | bytes 2048 | tf_op jit(solution)/shard_map/psum | solution.py:26
  37.2 1.6 fusion.25
  38.8 0.0 all-gather.3.cloned.1.call-update
  38.8 0.0 all-gather.5.cloned.1.call-start
  38.8 56.4 %all-gather.3.cloned.1.call-done = bf16[2,128,4096]{2,1,0:T(8,128)(2,1)} async-done(((bf16[2,128,128]{2,1,0:T(8,128)(2,1)}), bf16[2,128,4096]{2,1,0:T(8,128)(2,1)}) %all-gather.3.cloned.1.call-update) | async-done | bytes 2097168 | tf_op jit(solution)/shard_map/all_gather | solution.py:32
  95.2 0.0 copy-done
  95.2 3.0 fusion.42
  98.2 0.0 all-gather.5.cloned.1.call-update
  98.2 0.0 all-reduce.3.cloned.1.call-start
  98.2 32.8 %all-gather.5.cloned.1.call-done = bf16[2,1024,256]{2,1,0:T(8,128)(2,1)} async-done(((bf16[2,128,256]{2,1,0:T(8,128)(2,1)}), bf16[2,1024,256]{2,1,0:T(8,128)(2,1)}) %all-gather.5.cloned.1.call-update) | async-done | bytes 1048592 | tf_op jit(solution)/shard_map/all_gather | solution.py:36
  131.1 1.5 convert_reduce_fusion
  132.6 2.1 multiply_reduce_fusion
  134.7 1.3 copy-done.2
  136.0 0.0 copy-done.1
  136.0 1.5 fusion.10
  137.5 0.0 all-reduce.3.cloned.1.call-update
  137.5 0.0 reduce-scatter.5.cloned.1.call-start
  137.6 1.3 fusion.41
  138.8 1.3 fusion.37
  140.2 115.7 %all-reduce.3.cloned.1.call-done = f32[2,128,1024]{2,1,0:T(8,128)} async-done(((f32[2,128,1024]{2,1,0:T(8,128)}), f32[2,128,1024]{2,1,0:T(8,128)}) %all-reduce.3.cloned.1.call-update) | async-done | bytes 1048592 | tf_op jit(solution)/shard_map/psum | solution.py:48
  255.9 2.4 fusion.43
  258.3 13.7 %psum.53 = f32[2,256]{1,0:T(2,128)S(1)} all-reduce(f32[2,256]{1,0:T(2,128)S(1)} %get-tuple-element.23), channel_id=1, replica_groups=mesh['batch'=8,'col'=32] {'batch'}, use_global_device_ids=true, to_apply=%region_14.15 | all-reduce | flops 512 | bytes 4096 | tf_op jit(solution)/shard_map/psum | solution.py:58
  272.0 0.0 copy-done.5
  272.0 1.0 fusion.13
  272.9 2.7 convolution_bitcast_fusion
  275.7 0.0 reduce-scatter.5.cloned.1.call-update
  275.7 0.0 reduce-scatter.3.cloned.1.call-start
  275.7 4.3 convolution_bitcast_fusion.1
  280.0 0.0 reduce-scatter.3.cloned.1.call-update
  281.4 0.6 multiply_reduce_fusion.4
  282.7 0.0 copy-done.4
  282.7 0.9 multiply_reduce_fusion.2
  284.2 78.4 %psum.52 = f32[]{:T(128)} all-reduce(f32[]{:T(128)S(6)} %add.83), channel_id=1, replica_groups=mesh['batch'=8,'col'=32] {'batch','col'}, use_global_device_ids=true, to_apply=%region_12.13 | all-reduce | flops 1 | bytes 8 | tf_op jit(solution)/shard_map/psum | solution.py:69
  362.6 1.7 reduce-scatter.5.cloned.1.call-done
  364.4 0.0 copy-done.3
  364.4 0.0 copy-done.6
  364.4 0.0 copy-done.7
  364.4 1.0 fusion.39
  365.4 14.1 %all-reduce = (f32[2,128]{1,0:T(2,128)S(1)}, f32[2,128]{1,0:T(2,128)S(1)}) all-reduce(f32[2,128]{1,0:T(2,128)S(1)} %get-tuple-element.8, f32[2,128]{1,0:T(2,128)S(1)} %get-tuple-element.7), channel_id=1, replica_groups=mesh['batch'=8,'col'=32] {'batch'}, use_global_device_ids=true, to_apply=%region_18.19 | all-reduce | flops 512 | bytes 4096 | tf_op jit(solution)/shard_map/psum | solution.py:84
  379.5 0.5 reduce_sum.137
  380.1 0.5 broadcast_multiply_fusion.3
  380.6 0.7 fusion.31
  381.3 42.5 %reduce-scatter.3.cloned.1.call-done = f32[512,256]{1,0:T(8,128)} async-done(((f32[4096,256]{1,0:T(8,128)}), f32[512,256]{1,0:T(8,128)}) %reduce-scatter.3.cloned.1.call-update) | async-done | bytes 524304 | tf_op jit(solution)/shard_map/reduce_scatter | solution.py:77
  (11 shorter events, 0.0 us)
Async XLA Ops:
  7.2 88.0 %copy-start = (bf16[4096,256]{1,0:T(8,128)(2,1)S(1)}, bf16[4096,256]{1,0:T(8,128)(2,1)}, u32[]{:S(2)}) copy-start(bf16[4096,256]{1,0:T(8,128)(2,1)} %param.7) | copy-start | bytes 6291460
  7.2 88.0 %all-gather.3.cloned.1.call-start = ((), (), s32[]{:S(2)}) async-start(), calls=%async_computation.2 | async-start | bytes 2162688 | tf_op jit(solution)/shard_map/all_gather | solution.py:32
  38.8 92.3 %all-gather.5.cloned.1.call-start = ((), (), s32[]{:S(2)}) async-start(), calls=%async_computation.3 | async-start | bytes 1179648 | tf_op jit(solution)/shard_map/all_gather | solution.py:36
  98.2 157.7 %all-reduce.3.cloned.1.call-start = ((), (), s32[]{:S(2)}) async-start(), calls=%async_computation.4 | async-start | bytes 2097152 | tf_op jit(solution)/shard_map/psum | solution.py:48
  131.1 5.0 %copy-start.1 = (bf16[2,1024,256]{2,1,0:T(8,128)(2,1)S(1)}, bf16[2,1024,256]{2,1,0:T(8,128)(2,1)}, u32[]{:S(2)}) copy-start(bf16[2,1024,256]{2,1,0:T(8,128)(2,1)} %all-gather.5.cloned.1.call-done) | copy-start | bytes 3145732
  134.6 1.4 copy-start.2
  137.5 226.9 %reduce-scatter.5.cloned.1.call-start = ((), (), s32[]{:S(2)}) async-start(), calls=%async_computation.6 | async-start | bytes 4325376 | tf_op jit(solution)/shard_map/reduce_scatter | solution.py:70
  138.8 133.1 %copy-start.5 = (f32[1,128,256]{2,1,0:T(8,128)S(1)}, f32[1,128,256]{2,1,0:T(8,128)}, u32[]{:S(2)}) copy-start(f32[1,128,256]{2,1,0:T(8,128)} %get-tuple-element.13) | copy-start | bytes 393220
  275.7 148.1 %reduce-scatter.3.cloned.1.call-start = ((), (), s32[]{:S(2)}) async-start(), calls=%async_computation.5 | async-start | bytes 4718592 | tf_op jit(solution)/shard_map/reduce_scatter | solution.py:77
  280.0 2.7 copy-start.4
  280.0 84.3 %copy-start.3 = (bf16[2,128,128]{2,1,0:T(8,128)(2,1)S(1)}, bf16[2,128,128]{2,1,0:T(8,128)(2,1)}, u32[]{:S(2)}) copy-start(bf16[2,128,128]{2,1,0:T(8,128)(2,1)} %param.4) | copy-start | bytes 196612
  280.0 84.3 %copy-start.6 = (f32[128]{0:T(128)S(1)}, f32[128]{0:T(128)}, u32[]{:S(2)}) copy-start(f32[128]{0:T(128)} %param.5) | copy-start | bytes 1540
  280.0 84.3 %copy-start.7 = (f32[128]{0:T(128)S(1)}, f32[128]{0:T(128)}, u32[]{:S(2)}) copy-start(f32[128]{0:T(128)} %param.6) | copy-start | bytes 1540
Sparse Core Ops, SparseCore 0:
  38.9 56.2 all-gather.2
  98.3 32.7 all-gather.4
  137.6 118.2 all-reduce.2
  275.8 88.5 reduce-scatter.4
  367.3 56.3 reduce-scatter.2
where the time goes:
time: 431 us; the launch traced here: 430 us
  waiting for transfers between devices  249 us (58%)
  blocking collectives  134 us (31%)
  between operations  16.5 us (4%)
  other arithmetic  14.9 us (3%)
  matrix products  13.8 us (3%)
    psum x1, waiting for transfers between devices, shards(): kernel = lax.psum(kernel_part, 'col')  116 us
    psum x1, blocking collectives, shards(): loss = lax.psum(share, ('batch', 'col'))  78.4 us
    all_gather x1, waiting for transfers between devices, shards(): act_full = lax.all_gather(act, 'col', axis=2, tiled=True)  56.4 us
    reduce_scatter x1, waiting for transfers between devices, shards(): lax.psum_scatter(jnp.einsum('vrk,vrj->kj', act_full, dzb, preferred_eleme...  42.5 us
    all_gather x1, waiting for transfers between devices, shards(): z_all = lax.all_gather(z_local, 'batch', axis=1, tiled=True)  32.8 us
    psum x1, blocking collectives, shards(): total = lax.psum(jnp.sum(hidden_float, axis=1), 'batch')  17.3 us
    psum x1, blocking collectives, shards(): lax.psum((jnp.sum(preactivation_gradient, axis=1), jnp.sum(preactivation_...  14.1 us
    psum x1, blocking collectives, shards(): col_total = lax.psum(jnp.sum(summed, axis=1), 'batch')  13.7 us
  transfers between devices with their start and end apart: 5, of which 5 were waited for; matrix products, arithmetic and copies ran while one was open for 3% of the time, Pallas kernels for 0%

commit v1 on v0

--- a/solution.py
+++ b/solution.py
@@ -33,7 +33,14 @@
     z_local = jnp.einsum(
         "vrk,kj->vrj", act_full, weight, preferred_element_type=jnp.float32
     ).astype(jnp.bfloat16)
-    z_all = lax.all_gather(z_local, "batch", axis=1, tiled=True)
+    size = lax.axis_size("batch")
+    right = [(i, (i + 1) % size) for i in range(size)]
+    blocks = [z_local]
+    for reach in range(1, size):
+        blocks = [lax.ppermute(blocks[0], "batch", right), *blocks]
+    whole = jnp.concatenate(blocks, axis=1)
+    offset_2 = (lax.axis_index("batch") + 1) * blocks[-1].shape[1]
+    z_all = jnp.roll(whole, offset_2, axis=1)
     zf_all = z_all.astype(jnp.float32)
     zmean = jnp.mean(zf_all, axis=1, keepdims=True)
     zc_all = zf_all - zmean

time: 431 us -> 435 us (level)
  waiting for transfers between devices: 249 us -> 259 us
  other arithmetic: 14.9 us -> 9.55 us
    ppermute x0 -> x7, waiting for transfers between devices: none -> 38.1 us  [shards(): blocks = [lax.ppermute(blocks[0], 'batch', right), *blocks]]
    all_gather x1 -> x0, waiting for transfers between devices: 32.8 us -> none  [shards(): z_all = lax.all_gather(z_local, 'batch', axis=1, tiled=True)]
  transfers between devices with their start and end apart: 5 -> 11, of which waited for: 5 -> 11; matrix products, arithmetic and copies ran while one was open for 3% -> 2% of each run, Pallas kernels for 0% -> 0%
where the time goes in v1:
time: 435 us
  waiting for transfers between devices  259 us (60%)
  blocking collectives  134 us (31%)
  between operations  16.7 us (4%)
  matrix products  12.7 us (3%)
  other arithmetic  9.55 us (2%)
    psum x1, waiting for transfers between devices, shards(): kernel = lax.psum(kernel_part, 'col')  119 us
    psum x1, blocking collectives, shards(): loss = lax.psum(share, ('batch', 'col'))  78.4 us
    all_gather x1, waiting for transfers between devices, shards(): act_full = lax.all_gather(act, 'col', axis=2, tiled=True)  56.4 us
    reduce_scatter x1, waiting for transfers between devices, shards(): lax.psum_scatter(jnp.einsum('vrk,vrj->kj', act_full, dzb, preferred_eleme...  42.9 us
    ppermute x7, waiting for transfers between devices, shards(): blocks = [lax.ppermute(blocks[0], 'batch', right), *blocks]  38.1 us
    psum x1, blocking collectives, shards(): total = lax.psum(jnp.sum(hidden_float, axis=1), 'batch')  17.3 us
    psum x1, blocking collectives, shards(): col_total = lax.psum(jnp.sum(summed, axis=1), 'batch')  13.7 us
    psum x1, blocking collectives, shards(): lax.psum((jnp.sum(preactivation_gradient, axis=1), jnp.sum(preactivation_...  13.4 us
  transfers between devices with their start and end apart: 11, of which 11 were waited for; matrix products, arithmetic and copies ran while one was open for 2% of the time, Pallas kernels for 0%

profile of v1, /device:TPU:1, one launch (start us, length us, event | category | flops | bytes accessed | tf_op | source)
XLA Modules:
  0.0 434.6 jit_solution(4146744639509498059)
XLA Ops:
  7.2 0.0 copy-start
  7.2 0.0 all-gather.2.cloned.1.call-start
  7.2 1.0 convert_reduce_fusion.1
  8.2 17.3 %psum.49 = f32[2,128]{1,0:T(2,128)S(1)} all-reduce(f32[2,128]{1,0:T(2,128)S(1)} %convert_reduce_fusion.1), channel_id=1, replica_groups=mesh['batch'=8,'col'=32] {'batch'}, use_global_device_ids=true, to_apply=%region_1.0 | all-reduce | flops 256 | bytes 2048 | tf_op jit(solution)/shard_map/psum | solution.py:23
  25.5 0.9 fusion.32
  26.4 10.8 %psum.50 = f32[2,128]{1,0:T(2,128)S(1)} all-reduce(f32[2,128]{1,0:T(2,128)S(1)} %fusion.32), channel_id=1, replica_groups=mesh['batch'=8,'col'=32] {'batch'}, use_global_device_ids=true, to_apply=%region_3.0 | all-reduce | flops 256 | bytes 2048 | tf_op jit(solution)/shard_map/psum | solution.py:26
  37.2 1.6 fusion.25
  38.8 0.0 all-gather.2.cloned.1.call-update
  38.8 0.0 all-reduce.3.cloned.1.call-start
  38.8 56.4 %all-gather.2.cloned.1.call-done = bf16[2,128,4096]{2,1,0:T(8,128)(2,1)} async-done(((bf16[2,128,128]{2,1,0:T(8,128)(2,1)}), bf16[2,128,4096]{2,1,0:T(8,128)(2,1)}) %all-gather.2.cloned.1.call-update) | async-done | bytes 2097168 | tf_op jit(solution)/shard_map/all_gather | solution.py:32
  95.2 2.3 fusion.5
  97.5 1.4 collective-permute-start
  98.9 5.5 %collective-permute-done = bf16[2,128,256]{2,1,0:T(8,128)(2,1)S(1)} collective-permute-done((bf16[2,128,256]{2,1,0:T(8,128)(2,1)S(1)}, bf16[2,128,256]{2,1,0:T(8,128)(2,1)S(1)}, u32[]{:S(2)}, u32[]{:S(2)}) %collective-permute-start) | collective-permute-done | bytes 131104 | tf_op jit(solution)/shard_map/ppermute | solution.py:40
  104.3 5.5 %collective-permute-done.1 = bf16[2,128,256]{2,1,0:T(8,128)(2,1)S(1)} collective-permute-done((bf16[2,128,256]{2,1,0:T(8,128)(2,1)S(1)}, bf16[2,128,256]{2,1,0:T(8,128)(2,1)S(1)}, u32[]{:S(2)}, u32[]{:S(2)}) %collective-permute-start.1) | collective-permute-done | bytes 131104 | tf_op jit(solution)/shard_map/ppermute | solution.py:40
  109.8 5.0 %collective-permute-done.2 = bf16[2,128,256]{2,1,0:T(8,128)(2,1)S(1)} collective-permute-done((bf16[2,128,256]{2,1,0:T(8,128)(2,1)S(1)}, bf16[2,128,256]{2,1,0:T(8,128)(2,1)S(1)}, u32[]{:S(2)}, u32[]{:S(2)}) %collective-permute-start.2) | collective-permute-done | bytes 131104 | tf_op jit(solution)/shard_map/ppermute | solution.py:40
  114.8 0.0 collective-permute-start.3
  114.8 5.0 %collective-permute-done.3 = bf16[2,128,256]{2,1,0:T(8,128)(2,1)S(1)} collective-permute-done((bf16[2,128,256]{2,1,0:T(8,128)(2,1)S(1)}, bf16[2,128,256]{2,1,0:T(8,128)(2,1)S(1)}, u32[]{:S(2)}, u32[]{:S(2)}) %collective-permute-start.3) | collective-permute-done | bytes 131104 | tf_op jit(solution)/shard_map/ppermute | solution.py:40
  119.9 0.0 collective-permute-start.4
  119.9 5.0 %collective-permute-done.4 = bf16[2,128,256]{2,1,0:T(8,128)(2,1)S(1)} collective-permute-done((bf16[2,128,256]{2,1,0:T(8,128)(2,1)S(1)}, bf16[2,128,256]{2,1,0:T(8,128)(2,1)S(1)}, u32[]{:S(2)}, u32[]{:S(2)}) %collective-permute-start.4) | collective-permute-done | bytes 131104 | tf_op jit(solution)/shard_map/ppermute | solution.py:40
  124.9 5.8 %collective-permute-done.5 = bf16[2,128,256]{2,1,0:T(8,128)(2,1)S(1)} collective-permute-done((bf16[2,128,256]{2,1,0:T(8,128)(2,1)S(1)}, bf16[2,128,256]{2,1,0:T(8,128)(2,1)S(1)}, u32[]{:S(2)}, u32[]{:S(2)}) %collective-permute-start.5) | collective-permute-done | bytes 131104 | tf_op jit(solution)/shard_map/ppermute | solution.py:40
  130.7 6.3 %collective-permute-done.6 = bf16[2,128,256]{2,1,0:T(8,128)(2,1)S(1)} collective-permute-done((bf16[2,128,256]{2,1,0:T(8,128)(2,1)S(1)}, bf16[2,128,256]{2,1,0:T(8,128)(2,1)S(1)}, u32[]{:S(2)}, u32[]{:S(2)}) %collective-permute-start.6) | collective-permute-done | bytes 131104 | tf_op jit(solution)/shard_map/ppermute | solution.py:40
  137.3 0.2 convert_reduce_fusion
  137.5 0.3 multiply_reduce_fusion
  137.8 0.8 copy-done.1
  138.6 0.7 copy-done.2
  139.3 1.5 fusion.10
  140.7 0.0 all-reduce.3.cloned.1.call-update
  140.8 0.0 reduce-scatter.5.cloned.1.call-start
  140.8 0.6 fusion.37
  141.4 0.6 fusion.42
  142.0 119.5 %all-reduce.3.cloned.1.call-done = f32[2,128,1024]{2,1,0:T(8,128)} async-done(((f32[2,128,1024]{2,1,0:T(8,128)}), f32[2,128,1024]{2,1,0:T(8,128)}) %all-reduce.3.cloned.1.call-update) | async-done | bytes 1048592 | tf_op jit(solution)/shard_map/psum | solution.py:55
  261.5 2.0 fusion.43
  263.5 13.7 %psum.53 = f32[2,256]{1,0:T(2,128)S(1)} all-reduce(f32[2,256]{1,0:T(2,128)S(1)} %get-tuple-element.23), channel_id=1, replica_groups=mesh['batch'=8,'col'=32] {'batch'}, use_global_device_ids=true, to_apply=%region_14.15 | all-reduce | flops 512 | bytes 4096 | tf_op jit(solution)/shard_map/psum | solution.py:65
  277.2 2.7 convolution_bitcast_fusion
  280.0 0.0 reduce-scatter.5.cloned.1.call-update
  280.0 0.0 reduce-scatter.3.cloned.1.call-start
  280.0 4.3 convolution_bitcast_fusion.1
  284.3 0.0 reduce-scatter.3.cloned.1.call-update
  285.1 0.6 multiply_reduce_fusion.4
  287.0 0.9 multiply_reduce_fusion.2
  288.5 78.4 %psum.52 = f32[]{:T(128)} all-reduce(f32[]{:T(128)S(6)} %add.99), channel_id=1, replica_groups=mesh['batch'=8,'col'=32] {'batch','col'}, use_global_device_ids=true, to_apply=%region_12.13 | all-reduce | flops 1 | bytes 8 | tf_op jit(solution)/shard_map/psum | solution.py:76
  366.9 2.0 reduce-scatter.5.cloned.1.call-done
  368.9 1.0 fusion.40
  369.9 13.4 %all-reduce = (f32[2,128]{1,0:T(2,128)S(1)}, f32[2,128]{1,0:T(2,128)S(1)}) all-reduce(f32[2,128]{1,0:T(2,128)S(1)} %get-tuple-element.8, f32[2,128]{1,0:T(2,128)S(1)} %get-tuple-element.7), channel_id=1, replica_groups=mesh['batch'=8,'col'=32] {'batch'}, use_global_device_ids=true, to_apply=%region_18.19 | all-reduce | flops 512 | bytes 4096 | tf_op jit(solution)/shard_map/psum | solution.py:91
  383.4 0.5 reduce_sum.137
  383.9 0.5 broadcast_multiply_fusion.3
  384.4 0.7 fusion.31
  385.1 42.9 %reduce-scatter.3.cloned.1.call-done = f32[512,256]{1,0:T(8,128)} async-done(((f32[4096,256]{1,0:T(8,128)}), f32[512,256]{1,0:T(8,128)}) %reduce-scatter.3.cloned.1.call-update) | async-done | bytes 524304 | tf_op jit(solution)/shard_map/reduce_scatter | solution.py:84
  (36 shorter events, 0.3 us)
Async XLA Ops:
  7.2 88.0 %copy-start = (bf16[4096,256]{1,0:T(8,128)(2,1)S(1)}, bf16[4096,256]{1,0:T(8,128)(2,1)}, u32[]{:S(2)}) copy-start(bf16[4096,256]{1,0:T(8,128)(2,1)} %param.7) | copy-start | bytes 6291460
  7.2 88.0 %all-gather.2.cloned.1.call-start = ((), (), s32[]{:S(2)}) async-start(), calls=%async_computation.2 | async-start | bytes 2162688 | tf_op jit(solution)/shard_map/all_gather | solution.py:32
  38.8 222.7 %all-reduce.3.cloned.1.call-start = ((), (), s32[]{:S(2)}) async-start(), calls=%async_computation.3 | async-start | bytes 2097152 | tf_op jit(solution)/shard_map/psum | solution.py:55
  97.5 6.8 %collective-permute-start = (bf16[2,128,256]{2,1,0:T(8,128)(2,1)S(1)}, bf16[2,128,256]{2,1,0:T(8,128)(2,1)S(1)}, u32[]{:S(2)}, u32[]{:S(2)}) collective-permute-start(bf16[2,128,256]{2,1,0:T(8,128)(2,1)S(1)} %fusion.5), channel_id=1, source_target_pairs={{0,32},{32,64},{64,96},{96,128},{128,160},{160,192},{192,224},{224... | collective-permute-start | bytes 393224 | tf_op jit(solution)/shard_map/ppermute | solution.py:40
  104.3 5.5 %collective-permute-start.1 = (bf16[2,128,256]{2,1,0:T(8,128)(2,1)S(1)}, bf16[2,128,256]{2,1,0:T(8,128)(2,1)S(1)}, u32[]{:S(2)}, u32[]{:S(2)}) collective-permute-start(bf16[2,128,256]{2,1,0:T(8,128)(2,1)S(1)} %collective-permute-done), channel_id=1, source_target_pairs={{0,32},{32,64},{64,96},{96,128},{128,160},{160,192},{192,224},{224... | collective-permute-start | bytes 393224 | tf_op jit(solution)/shard_map/ppermute | solution.py:40
  109.8 5.0 %collective-permute-start.2 = (bf16[2,128,256]{2,1,0:T(8,128)(2,1)S(1)}, bf16[2,128,256]{2,1,0:T(8,128)(2,1)S(1)}, u32[]{:S(2)}, u32[]{:S(2)}) collective-permute-start(bf16[2,128,256]{2,1,0:T(8,128)(2,1)S(1)} %collective-permute-done.1), channel_id=1, source_target_pairs={{0,32},{32,64},{64,96},{96,128},{128,160},{160,192},{192,224},{224... | collective-permute-start | bytes 393224 | tf_op jit(solution)/shard_map/ppermute | solution.py:40
  114.8 5.0 %collective-permute-start.3 = (bf16[2,128,256]{2,1,0:T(8,128)(2,1)S(1)}, bf16[2,128,256]{2,1,0:T(8,128)(2,1)S(1)}, u32[]{:S(2)}, u32[]{:S(2)}) collective-permute-start(bf16[2,128,256]{2,1,0:T(8,128)(2,1)S(1)} %collective-permute-done.2), channel_id=1, source_target_pairs={{0,32},{32,64},{64,96},{96,128},{128,160},{160,192},{192,224},{224... | collective-permute-start | bytes 393224 | tf_op jit(solution)/shard_map/ppermute | solution.py:40
  119.9 5.0 %collective-permute-start.4 = (bf16[2,128,256]{2,1,0:T(8,128)(2,1)S(1)}, bf16[2,128,256]{2,1,0:T(8,128)(2,1)S(1)}, u32[]{:S(2)}, u32[]{:S(2)}) collective-permute-start(bf16[2,128,256]{2,1,0:T(8,128)(2,1)S(1)} %collective-permute-done.3), channel_id=1, source_target_pairs={{0,32},{32,64},{64,96},{96,128},{128,160},{160,192},{192,224},{224... | collective-permute-start | bytes 393224 | tf_op jit(solution)/shard_map/ppermute | solution.py:40
  124.9 5.8 %collective-permute-start.5 = (bf16[2,128,256]{2,1,0:T(8,128)(2,1)S(1)}, bf16[2,128,256]{2,1,0:T(8,128)(2,1)S(1)}, u32[]{:S(2)}, u32[]{:S(2)}) collective-permute-start(bf16[2,128,256]{2,1,0:T(8,128)(2,1)S(1)} %collective-permute-done.4), channel_id=1, source_target_pairs={{0,32},{32,64},{64,96},{96,128},{128,160},{160,192},{192,224},{224... | collective-permute-start | bytes 393224 | tf_op jit(solution)/shard_map/ppermute | solution.py:40
  130.7 6.3 %collective-permute-start.6 = (bf16[2,128,256]{2,1,0:T(8,128)(2,1)S(1)}, bf16[2,128,256]{2,1,0:T(8,128)(2,1)S(1)}, u32[]{:S(2)}, u32[]{:S(2)}) collective-permute-start(bf16[2,128,256]{2,1,0:T(8,128)(2,1)S(1)} %collective-permute-done.5), channel_id=1, source_target_pairs={{0,32},{32,64},{64,96},{96,128},{128,160},{160,192},{192,224},{224... | collective-permute-start | bytes 393224 | tf_op jit(solution)/shard_map/ppermute | solution.py:40
  137.3 1.3 copy-start.1
  137.8 1.5 copy-start.2
  140.8 228.1 %reduce-scatter.5.cloned.1.call-start = ((), (), s32[]{:S(2)}) async-start(), calls=%async_computation.5 | async-start | bytes 4325376 | tf_op jit(solution)/shard_map/reduce_scatter | solution.py:77
  280.0 148.1 %reduce-scatter.3.cloned.1.call-start = ((), (), s32[]{:S(2)}) async-start(), calls=%async_computation.4 | async-start | bytes 4718592 | tf_op jit(solution)/shard_map/reduce_scatter | solution.py:84
  284.3 2.7 copy-start.4
  284.3 84.6 %copy-start.3 = (bf16[2,128,128]{2,1,0:T(8,128)(2,1)S(1)}, bf16[2,128,128]{2,1,0:T(8,128)(2,1)}, u32[]{:S(2)}) copy-start(bf16[2,128,128]{2,1,0:T(8,128)(2,1)} %param.4) | copy-start | bytes 196612
  284.3 84.6 %copy-start.5 = (f32[128]{0:T(128)S(1)}, f32[128]{0:T(128)}, u32[]{:S(2)}) copy-start(f32[128]{0:T(128)} %param.5) | copy-start | bytes 1540
  284.3 84.6 %copy-start.6 = (f32[128]{0:T(128)S(1)}, f32[128]{0:T(128)}, u32[]{:S(2)}) copy-start(f32[128]{0:T(128)} %param.6) | copy-start | bytes 1540
Sparse Core Ops, SparseCore 0:
  38.9 56.2 all-gather.1
  140.9 120.5 all-reduce.2
  280.1 88.7 reduce-scatter.4
  371.9 56.1 reduce-scatter.2
